TPU v7x, 256 devices: a whole 4x4x8 slice. The times are simulated.
256 devices in a mesh: star: 64 (over y, z_lo, x, core), gas: 4 (over z_hi).
Axes of the slice: x: 4, y: 4, z: 8 (z_hi: 4, z_lo: 2; z = z_hi * 2 + z_lo), core: 2. Of those that a mesh axis runs over, the one named last changes fastest.
Arguments:
- star_pos: float32 [3, 131072], P(None, ('star', 'gas')), may hold values from 0 to 32
- star_vel: float32 [3, 131072], P(None, ('star', 'gas')), may hold values from -6 to 6
- star_accel: float32 [6, 131072], P(None, ('star', 'gas')), may hold values from -6 to 6
- star_mass: float32 [131072], P(('star', 'gas')), may hold values from 0.1 to 2
- active: int32 [2048], replicated, may hold values from 0 to 131071, as said below
- density: float32 [256, 32, 64], P('star', 'gas'), may hold values from 0.5 to 4
- flow_in: float32 [3, 256, 32, 64], P(None, 'star', 'gas'), may hold values from -2 to 2
- field_in: float32 [3, 256, 32, 64], P(None, 'star', 'gas'), may hold values from -4 to 4
Outputs:
- star_new: float32 [12, 131072], P(None, ('star', 'gas'))
- flow: float32 [3, 256, 32, 64], P(None, 'star', 'gas')
- field_out: float32 [3, 256, 32, 64], P(None, 'star', 'gas')
Inputs may be any that keep to these rules, and one draw needn't show every extreme that they name: Distinct and increasing; among the 512 consecutive indices of one device at most 24 are active, and in every draw some device holds exactly 24.
All inputs are finite; a program needn't handle non-finite values.
Results may differ from a plain program's by a relative error of at most 0.0001.
Values sent between devices are 32-bit elements; how exact they have to be, the bound alone decides.
A program may use at most 64 MiB of HBM per device.

v0:
```python
import math
import jax
import jax.numpy as jnp
from jax import lax
from jax.sharding import PartitionSpec as P

MOST = 24
gravity = 0.02
soften = 4.0
time_step = 1.5
field_step = 0.1
highest = lax.Precision.HIGHEST


def with_halo(block, sides, width):
    for axis, dim in sides:
        count = lax.axis_size(axis)
        forward = [(i, i + 1) for i in range(count - 1)]
        forward.append((count - 1, 0))
        backward = [(target, source) for source, target in forward]
        low = lax.ppermute(
            lax.slice_in_dim(block, block.shape[dim] - width, None, axis=dim), axis, forward
        )
        high = lax.ppermute(lax.slice_in_dim(block, 0, width, axis=dim), axis, backward)
        block = jnp.concatenate([low, block, high], axis=dim)
    return block


def grad_x(values):
    return 0.5 * (values[2:, 1:-1] - values[:-2, 1:-1])


def grad_y(values):
    return 0.5 * (values[1:-1, 2:] - values[1:-1, :-2])


def grad_z(values):
    return 0.5 * (jnp.roll(values, -1, 2) - jnp.roll(values, 1, 2))[1:-1, 1:-1]


def trim_rim(values):
    return values[1:-1, 1:-1]


def curl_of(comp_a, comp_b, comp_c):
    return (
        grad_y(comp_c) - grad_z(comp_b),
        grad_z(comp_a) - grad_x(comp_c),
        grad_x(comp_b) - grad_y(comp_a),
    )


def cross_of(lhs_vec, rhs_vec):
    return (
        lhs_vec[1] * rhs_vec[2] - lhs_vec[2] * rhs_vec[1],
        lhs_vec[2] * rhs_vec[0] - lhs_vec[0] * rhs_vec[2],
        lhs_vec[0] * rhs_vec[1] - lhs_vec[1] * rhs_vec[0],
    )


def field_rate(padded_field, padded_flow, padded_density):
    current = curl_of(padded_field[0], padded_field[1], padded_field[2])
    inner_field = (trim_rim(padded_field[0]), trim_rim(padded_field[1]), trim_rim(padded_field[2]))
    inner_flow = (trim_rim(padded_flow[0]), trim_rim(padded_flow[1]), trim_rim(padded_flow[2]))
    resist = trim_rim(padded_density) ** (-1.5)
    lorentz = cross_of(current, inner_field)
    drift = cross_of(lorentz, inner_field)
    motion = cross_of(inner_flow, inner_field)
    emf_a = motion[0] + resist * drift[0]
    emf_b = motion[1] + resist * drift[1]
    emf_c = motion[2] + resist * drift[2]
    return jnp.stack(curl_of(emf_a, emf_b, emf_c))


def pair_terms(target, resident, cell_place, cell_mass):
    star_gap = resident[0:3, None, :] - target[0:3, :, None]
    rel_vel = resident[3:6, None, :] - target[3:6, :, None]
    inv_r = lax.rsqrt(jnp.sum(star_gap * star_gap, 0) + soften)
    weight = gravity * resident[6][None, :] * inv_r * inv_r * inv_r
    star_acc = jnp.sum(weight[None] * star_gap, 2)
    approach = jnp.sum(star_gap * rel_vel, 0)
    star_jerk = jnp.sum(
        weight[None] * (rel_vel - 3.0 * (approach * inv_r * inv_r)[None] * star_gap), 2
    )
    cell_gap = cell_place[:, None, :] - target[0:3, :, None]
    inv_g = lax.rsqrt(jnp.sum(cell_gap * cell_gap, 0) + soften)
    inv_cube = gravity * inv_g * inv_g * inv_g
    gas_acc = jnp.sum((inv_cube * cell_mass[None, :])[None] * cell_gap, 2)
    cell_kick = -jnp.sum((inv_cube * target[6][:, None])[None] * cell_gap, 1)
    return (jnp.concatenate([star_acc + gas_acc, star_jerk], 0), cell_kick)


def all_terms(targets, resident, cell_place, cell_mass):
    target_total = targets.shape[1]
    block_width = math.gcd(target_total, 64)
    blocks = targets.reshape(7, target_total // block_width, block_width).transpose(1, 0, 2)

    def one_block(running, target_block):
        terms_here, cell_kick = pair_terms(target_block, resident, cell_place, cell_mass)
        return (running + cell_kick, terms_here)

    kick_sum, block_terms = lax.scan(one_block, jnp.zeros(cell_place.shape, jnp.float32), blocks)
    return (block_terms.transpose(1, 0, 2).reshape(6, target_total), kick_sum)


def body(star_pos, star_vel, star_accel, star_mass, active, density, flow_in, field_in):
    resident_total = star_pos.shape[1]
    old_acc = star_accel[0:3]
    old_jerk = star_accel[3:6]
    pred_pos = (
        star_pos
        + time_step * star_vel
        + time_step**2 / 2.0 * old_acc
        + time_step**3 / 6.0 * old_jerk
    )
    pred_vel = star_vel + time_step * old_acc + time_step**2 / 2.0 * old_jerk
    resident = jnp.concatenate([pred_pos, pred_vel, star_mass[None]], 0)
    my_rank = lax.axis_index("star") * lax.axis_size("gas") + lax.axis_index("gas")
    owner_of = active // resident_total
    local_slot = active % resident_total
    is_mine = owner_of == my_rank
    rows_iota = jnp.arange(resident_total, dtype=jnp.int32)
    owned = (is_mine[None, :] & (local_slot[None, :] == rows_iota[:, None])).astype(jnp.float32)
    active_mask = jnp.sum(owned, 1) > 0.5
    ext_x, ext_y, ext_z = density.shape
    grid_shape = (ext_x, ext_y, ext_z)
    coord_x = (lax.axis_index("star") * ext_x + jnp.arange(ext_x)).astype(jnp.float32) + 0.5
    coord_y = (lax.axis_index("gas") * ext_y + jnp.arange(ext_y)).astype(jnp.float32) + 0.5
    coord_z = jnp.arange(ext_z).astype(jnp.float32) + 0.5
    cell_place = jnp.stack(
        [
            jnp.broadcast_to(coord_x[:, None, None], grid_shape),
            jnp.broadcast_to(coord_y[None, :, None], grid_shape),
            jnp.broadcast_to(coord_z[None, None, :], grid_shape),
        ]
    ).reshape(3, -1)
    cell_mass = density.reshape(-1)
    order_rank = jnp.cumsum(is_mine.astype(jnp.int32)) - 1
    slot_iota = jnp.arange(MOST, dtype=jnp.int32)
    slot_pick = (is_mine[:, None] & (order_rank[:, None] == slot_iota[None, :])).astype(jnp.float32)
    selector = jnp.dot(owned, slot_pick, precision=highest)
    packed = jnp.dot(resident, selector, precision=highest)
    targets = lax.all_gather(packed, ("star", "gas"), axis=1, tiled=True)
    partial_terms, kick_sum = all_terms(targets, resident, cell_place, cell_mass)
    summed = lax.psum(partial_terms, ("star", "gas"))
    mine_terms = lax.dynamic_slice_in_dim(summed, my_rank * MOST, MOST, 1)
    own_terms = jnp.dot(mine_terms, selector.T, precision=highest)
    new_acc = own_terms[0:3]
    new_jerk = own_terms[3:6]
    vel_one = (
        star_vel
        + time_step * (old_acc + new_acc) / 2.0
        + time_step**2 * (old_jerk - new_jerk) / 12.0
    )
    pos_one = (
        star_pos
        + time_step * (star_vel + vel_one) / 2.0
        + time_step**2 * (old_acc - new_acc) / 12.0
    )
    updated = jnp.concatenate([pos_one, vel_one, new_acc, new_jerk], 0)
    base = jnp.concatenate([star_pos, star_vel, star_accel], 0)
    star_new = jnp.where(active_mask[None, :], updated, base)
    flow = flow_in + time_step * kick_sum.reshape(3, ext_x, ext_y, ext_z)

    def rate_of(values):
        padded = with_halo(
            jnp.concatenate([values, flow, density[None]], 0), (("star", 1), ("gas", 2)), 2
        )
        return field_rate(padded[0:3], padded[3:6], padded[6])

    first_section = field_in + field_step * rate_of(field_in)
    field_out = 0.5 * (field_in + first_section + field_step * rate_of(first_section))
    return (star_new, flow, field_out)


def solution(mesh):
    placed = (
        P(None, ("star", "gas")),
        P(None, ("star", "gas")),
        P(None, ("star", "gas")),
        P(("star", "gas")),
        P(),
        P("star", "gas", None),
        P(None, "star", "gas", None),
        P(None, "star", "gas", None),
    )
    return jax.shard_map(
        body,
        mesh=mesh,
        in_specs=placed,
        out_specs=(
            P(None, ("star", "gas")),
            P(None, "star", "gas", None),
            P(None, "star", "gas", None),
        ),
        check_vma=False,
    )
```

profile of v0, /device:TPU:1, one launch (start us, length us, event | category | flops | bytes accessed | tf_op | source)
XLA Modules:
  0.0 1057.4 jit_solution(8387592304197424626)
XLA Ops:
  7.3 0.7 add_select_fusion
  8.0 0.7 convert_bitcast_fusion
  9.3 1.4 fusion.14
  10.9 629.3 %all-gather = f32[256,24,7]{1,2,0:T(8,128)S(1)} all-gather(f32[1,24,7]{1,2,0:T(8,128)S(1)} %convolution_bitcast_fusion), channel_id=1, replica_groups=mesh['star'=64,'gas'=4] {'star','gas'}, dimensions={0}, use_global_device_ids=true | all-gather | bytes 172704 | tf_op jit(solution)/shard_map/all_gather | solution.py:143
  640.4 0.5 reshape.159
  641.8 144.5 %while.14 = (s32[]{:T(128)}, f32[3,2048]{1,0:T(4,128)S(1)}, f32[96,6,64]{2,1,0:T(8,128)S(1)}, f32[3,4,8,64]{3,2,1,0:T(8,128)}, f32[96,7,64]{2,0,1:T(8,128)S(1)},...) while((s32[]{:T(128)}, f32[3,2048]{1,0:T(4,128)S(1)}, ...), condition=%wide.wide.region_11.12_spmd.clone, body=%wide.wide.region_3.11_spmd.clone.sunk | while | flops 5353989 | bytes 4405187 | solution.py:102
  642.8 0.5 fusion.148
  644.3 0.5 fusion.148
  645.8 0.5 fusion.148
  647.3 0.5 fusion.148
  648.8 0.5 fusion.148
  650.3 0.5 fusion.148
  651.8 0.5 fusion.148
  653.3 0.5 fusion.148
  654.8 0.5 fusion.148
  656.3 0.5 fusion.148
  657.8 0.5 fusion.148
  659.3 0.5 fusion.148
  660.8 0.5 fusion.148
  662.3 0.5 fusion.148
  663.8 0.5 fusion.148
  666.8 0.5 fusion.148
  668.3 0.5 fusion.148
  669.9 0.5 fusion.148
  671.4 0.5 fusion.148
  672.9 0.5 fusion.148
  674.4 0.5 fusion.148
  675.9 0.5 fusion.148
  677.4 0.5 fusion.148
  678.9 0.5 fusion.148
  680.4 0.5 fusion.148
  681.9 0.5 fusion.148
  683.4 0.5 fusion.148
  684.9 0.5 fusion.148
  786.5 0.7 pad_maximum_fusion.9
  787.4 6.9 collective-permute-start.1
  794.3 0.8 reshape.156
  795.1 0.8 convert_reduce_fusion
  796.1 3.6 collective-permute-start.3
  799.7 1.9 collective-permute-done.2
  802.8 7.0 collective-permute-start.5
  809.8 231.5 %all-reduce.2.cloned.1.call-done = f32[6,6144]{1,0:T(8,128)} async-done(((f32[6,6144]{1,0:T(8,128)}), f32[6,6144]{1,0:T(8,128)}) %all-reduce.2.cloned.1.call-update) | async-done | bytes 147472 | tf_op jit(solution)/shard_map/psum | solution.py:145
  1041.2 0.9 fusion.97
  1042.2 0.9 collective-permute-start.6
  1043.1 2.7 collective-permute-start.7
  1045.9 0.6 maximum_select_fusion
  1046.5 2.1 collective-permute-done.6
  1049.9 0.6 fusion.58
  (1313 shorter events, 127.1 us)
Async XLA Ops:
  7.2 1034.1 %all-reduce.2.cloned.1.call-start = ((), (), s32[]{:S(2)}) async-start(), calls=%async_computation | async-start | bytes 393216 | tf_op jit(solution)/shard_map/psum | solution.py:145
  9.3 1.4 copy-start.5
  9.3 1.4 copy-start.7
  9.3 1.4 copy-start.8
  9.3 1.5 copy-start.6
  640.3 1.0 copy-start.2
  641.2 0.6 copy-start.4
  641.8 144.7 %copy-start.9 = (f32[3,4,8,64]{3,2,1,0:T(8,128)S(1)}, f32[3,4,8,64]{3,2,1,0:T(8,128)}, u32[]{:S(2)}) copy-start(f32[3,4,8,64]{3,2,1,0:T(8,128)} %param.16) | copy-start | bytes 73732
  641.8 144.7 %copy-start.1 = (f32[3,4,8,64]{3,2,1,0:T(8,128)S(1)}, f32[3,4,8,64]{3,2,1,0:T(8,128)}, u32[]{:S(2)}) copy-start(f32[3,4,8,64]{3,2,1,0:T(8,128)} %param.17) | copy-start | bytes 73732
  786.4 9.5 copy-start.3
  786.5 262.1 %copy-start = (f32[3,4,8,64]{3,2,1,0:T(8,128)}, f32[3,4,8,64]{3,2,1,0:T(8,128)S(1)}, u32[]{:S(2)}) copy-start(f32[3,4,8,64]{3,2,1,0:T(8,128)S(1)} %add.174) | copy-start | bytes 73732
  787.3 8.6 collective-permute-start
  787.4 8.5 collective-permute-start.1
  796.0 5.5 collective-permute-start.2
  796.1 5.4 collective-permute-start.3
  802.7 239.5 %collective-permute-start.4 = (f32[7,2,8,64]{3,2,1,0:T(8,128)S(1)}, f32[7,2,8,64]{3,2,1,0:T(8,128)S(1)}, u32[]{:S(2)}, u32[]{:S(2)}) collective-permute-start(f32[7,2,8,64]{3,2,1,0:T(8,128)S(1)} %get-tuple-element.178), channel_id=1, source_target_pairs={{0,4},{4,8},{8,12},{12,16},{16,20},{20,24},{24,28},{28,32},{32,36}... | collective-permute-start | bytes 86024 | tf_op jit(solution)/shard_map/ppermute | solution.py:21
  802.8 239.4 %collective-permute-start.5 = (f32[7,2,8,64]{3,2,1,0:T(8,128)S(1)}, f32[7,2,8,64]{3,2,1,0:T(8,128)S(1)}, u32[]{:S(2)}, u32[]{:S(2)}) collective-permute-start(f32[7,2,8,64]{3,2,1,0:T(8,128)S(1)} %get-tuple-element.179), channel_id=1, source_target_pairs={{4,0},{8,4},{12,8},{16,12},{20,16},{24,20},{28,24},{32,28},{36,32}... | collective-permute-start | bytes 86024 | tf_op jit(solution)/shard_map/ppermute | solution.py:24
  1042.2 6.4 collective-permute-start.6
  1043.1 5.5 collective-permute-start.7
Sparse Core Ops, SparseCore 0:
  795.3 245.9 all-reduce.1
where the time goes:
time: 1060 us
  blocking collectives  629 us (59%)
  waiting for transfers between devices  235 us (22%)
  other arithmetic  139 us (13%)
  starting transfers between devices  21.4 us (2%)
  between operations  14.4 us (1%)
    all_gather x1, blocking collectives, body(): targets = lax.all_gather(packed, ('star', 'gas'), axis=1, tiled=True)  629 us
    psum x1, waiting for transfers between devices, body(): summed = lax.psum(partial_terms, ('star', 'gas'))  231 us
    reduce_sum x96, other arithmetic, pair_terms(): gas_acc = jnp.sum((inv_cube * cell_mass[None, :])[None] * cell_gap, 2)  48.2 us
    reduce_sum x96, other arithmetic, pair_terms(): star_acc = jnp.sum(weight[None] * star_gap, 2)  27.3 us
  transfers between devices with their start and end apart: 9, of which 3 were waited for; matrix products, arithmetic and copies ran while one was open for 0% of the time, Pallas kernels for 0%

commit v1 on v0

--- a/solution.py
+++ b/solution.py
@@ -140,7 +140,10 @@
     slot_pick = (is_mine[:, None] & (order_rank[:, None] == slot_iota[None, :])).astype(jnp.float32)
     selector = jnp.dot(owned, slot_pick, precision=highest)
     packed = jnp.dot(resident, selector, precision=highest)
-    targets = lax.all_gather(packed, ("star", "gas"), axis=1, tiled=True)
+    targets = jnp.concatenate(
+        lax.all_to_all(jnp.stack([packed] * lax.axis_size(("star", "gas"))), ("star", "gas"), 0, 0),
+        axis=1,
+    )
     partial_terms, kick_sum = all_terms(targets, resident, cell_place, cell_mass)
     summed = lax.psum(partial_terms, ("star", "gas"))
     mine_terms = lax.dynamic_slice_in_dim(summed, my_rank * MOST, MOST, 1)

time: 1060 us -> 468 us (0.44)
  blocking collectives: 629 us -> 0 us
  waiting for transfers between devices: 235 us -> 263 us
    all_gather x1 -> x0, blocking collectives: 629 us -> none  [body(): targets = lax.all_gather(packed, ('star', 'gas'), axis=1, tiled=True)]
    all_to_all x0 -> x1, starting transfers between devices: none -> 15.6 us  [body(): lax.all_to_all(jnp.stack([packed] * lax.axis_size(('star', 'gas'))), ('st...]
    all_to_all x0 -> x1, waiting for transfers between devices: none -> 14.8 us  [body(): lax.all_to_all(jnp.stack([packed] * lax.axis_size(('star', 'gas'))), ('st...]
    ppermute x4, starting transfers between devices: 20.2 us -> 8.01 us  [with_halo(): lax.ppermute(lax.slice_in_dim(block, 0, width, axis=dim), axis, backward)]
    psum x1, waiting for transfers between devices: 231 us -> 242 us  [body(): summed = lax.psum(partial_terms, ('star', 'gas'))]
  transfers between devices with their start and end apart: 9 -> 10, of which waited for: 3 -> 7; matrix products, arithmetic and copies ran while one was open for 0% -> 1% of each run, Pallas kernels for 0% -> 0%
where the time goes in v1:
time: 468 us
  waiting for transfers between devices  263 us (56%)
  other arithmetic  141 us (30%)
  starting transfers between devices  29.3 us (6%)
  between operations  14.4 us (3%)
  local copies, waits for them, and re-layouts  8.64 us (2%)
  loops' own time  8.23 us (2%)
    psum x1, waiting for transfers between devices, body(): summed = lax.psum(partial_terms, ('star', 'gas'))  242 us
    reduce_sum x96, other arithmetic, pair_terms(): gas_acc = jnp.sum((inv_cube * cell_mass[None, :])[None] * cell_gap, 2)  48.2 us
    reduce_sum x96, other arithmetic, pair_terms(): star_acc = jnp.sum(weight[None] * star_gap, 2)  27.3 us
    reduce_sum x96, other arithmetic, pair_terms(): inv_g = lax.rsqrt(jnp.sum(cell_gap * cell_gap, 0) + soften)  21.1 us
    all_to_all x1, starting transfers between devices, body(): lax.all_to_all(jnp.stack([packed] * lax.axis_size(('star', 'gas'))), ('st...  15.6 us
    all_to_all x1, waiting for transfers between devices, body(): lax.all_to_all(jnp.stack([packed] * lax.axis_size(('star', 'gas'))), ('st...  14.8 us
    mul x96, other arithmetic, pair_terms(): cell_kick = -jnp.sum((inv_cube * target[6][:, None])[None] * cell_gap, 1)  14.6 us
    reduce_sum x96, other arithmetic, pair_terms(): inv_r = lax.rsqrt(jnp.sum(star_gap * star_gap, 0) + soften)  13.4 us
  transfers between devices with their start and end apart: 10, of which 7 were waited for; matrix products, arithmetic and copies ran while one was open for 1% of the time, Pallas kernels for 0%

profile of v1, /device:TPU:1, one launch (start us, length us, event | category | flops | bytes accessed | tf_op | source)
XLA Modules:
  0.0 467.8 jit_solution(18409032793383858442)
XLA Ops:
  7.2 0.7 add_select_fusion
  7.9 0.7 convert_bitcast_fusion
  9.2 1.4 fusion.14
  10.9 1.4 reshape.161
  12.3 15.6 %all-to-all-start = ((f32[256,1,168]{2,1,0:T(1,128)}), f32[256,1,168]{2,1,0:T(1,128)S(1)}, u32[]{:S(2)}, u32[]{:S(2)}) async-start(f32[256,1,168]{2,1,0:T(1,128)} %reshape.161), calls=%async_computation | async-start | bytes 524288 | tf_op jit(solution)/shard_map/all_to_all | solution.py:144
  28.4 14.8 %all-to-all-done = f32[256,1,168]{2,1,0:T(1,128)S(1)} async-done(((f32[256,1,168]{2,1,0:T(1,128)}), f32[256,1,168]{2,1,0:T(1,128)S(1)}, u32[]{:S(2)}, u32[]{:S(2)}) %all-to-all-start) | async-done | bytes 172064 | tf_op jit(solution)/shard_map/all_to_all | solution.py:144
  43.2 0.5 broadcast.239
  43.7 1.3 reduce.2
  46.1 144.6 %while.14 = (s32[]{:T(128)}, f32[3,2048]{1,0:T(4,128)S(1)}, f32[96,6,64]{2,1,0:T(8,128)S(1)}, f32[3,4,8,64]{3,2,1,0:T(8,128)}, f32[96,7,64]{2,0,1:T(8,128)S(1)},...) while((s32[]{:T(128)}, f32[3,2048]{1,0:T(4,128)S(1)}, ...), condition=%wide.wide.region_11.12_spmd.clone, body=%wide.wide.region_3.11_spmd.clone.sunk | while | flops 5353989 | bytes 4405187 | solution.py:102
  47.0 0.5 fusion.149
  48.5 0.5 fusion.149
  50.0 0.5 fusion.149
  51.5 0.5 fusion.149
  53.0 0.5 fusion.149
  54.5 0.5 fusion.149
  56.1 0.5 fusion.149
  57.6 0.5 fusion.149
  59.1 0.5 fusion.149
  60.6 0.5 fusion.149
  63.6 0.5 fusion.149
  65.1 0.5 fusion.149
  66.6 0.5 fusion.149
  68.1 0.5 fusion.149
  69.6 0.5 fusion.149
  71.1 0.5 fusion.149
  72.6 0.5 fusion.149
  74.1 0.5 fusion.149
  75.6 0.5 fusion.149
  77.1 0.5 fusion.149
  78.6 0.5 fusion.149
  190.8 0.7 pad_maximum_fusion.9
  192.1 0.8 convert_reduce_fusion
  193.3 2.3 collective-permute-done.1
  195.6 0.7 fusion.31
  196.4 1.8 collective-permute-start.2
  198.3 1.8 collective-permute-start.3
  200.1 0.8 reshape.158
  200.9 0.7 collective-permute-done.2
  201.7 0.6 collective-permute-done.3
  203.5 2.4 collective-permute-start.4
  205.8 3.3 collective-permute-start.5
  209.2 242.5 %all-reduce.2.cloned.1.call-done = f32[6,6144]{1,0:T(8,128)} async-done(((f32[6,6144]{1,0:T(8,128)}), f32[6,6144]{1,0:T(8,128)}) %all-reduce.2.cloned.1.call-update) | async-done | bytes 147472 | tf_op jit(solution)/shard_map/psum | solution.py:148
  451.6 0.9 fusion.98
  452.7 0.9 collective-permute-start.6
  453.6 2.7 collective-permute-start.7
  456.3 0.6 maximum_select_fusion
  457.0 2.1 collective-permute-done.6
  460.3 0.6 fusion.58
  (1318 shorter events, 131.6 us)
Async XLA Ops:
  9.2 1.4 copy-start.5
  9.2 1.4 copy-start.7
  9.2 1.4 copy-start.8
  9.2 1.5 copy-start.6
  10.9 17.4 %copy-start.2 = (f32[4,8,64]{2,1,0:T(8,128)S(1)}, f32[4,8,64]{2,1,0:T(8,128)}, u32[]{:S(2)}) copy-start(f32[4,8,64]{2,1,0:T(8,128)} %param.15) | copy-start | bytes 24580
  12.3 30.9 %all-to-all-start = ((f32[256,1,168]{2,1,0:T(1,128)}), f32[256,1,168]{2,1,0:T(1,128)S(1)}, u32[]{:S(2)}, u32[]{:S(2)}) async-start(f32[256,1,168]{2,1,0:T(1,128)} %reshape.161), calls=%async_computation | async-start | bytes 524288 | tf_op jit(solution)/shard_map/all_to_all | solution.py:144
  28.0 423.7 %all-reduce.2.cloned.1.call-start = ((), (), s32[]{:S(2)}) async-start(), calls=%async_computation.1 | async-start | bytes 393216 | tf_op jit(solution)/shard_map/psum | solution.py:148
  28.2 17.3 %copy-start.4 = (f32[3,4,8,64]{3,2,1,0:T(8,128)}, f32[3,4,8,64]{3,2,1,0:T(8,128)S(1)}, u32[]{:S(2)}) copy-start(f32[3,4,8,64]{3,2,1,0:T(8,128)S(1)} %pad_maximum_fusion.20) | copy-start | bytes 73732
  46.0 144.7 %copy-start.9 = (f32[3,4,8,64]{3,2,1,0:T(8,128)S(1)}, f32[3,4,8,64]{3,2,1,0:T(8,128)}, u32[]{:S(2)}) copy-start(f32[3,4,8,64]{3,2,1,0:T(8,128)} %param.16) | copy-start | bytes 73732
  46.1 144.7 %copy-start.1 = (f32[3,4,8,64]{3,2,1,0:T(8,128)S(1)}, f32[3,4,8,64]{3,2,1,0:T(8,128)}, u32[]{:S(2)}) copy-start(f32[3,4,8,64]{3,2,1,0:T(8,128)} %param.17) | copy-start | bytes 73732
  190.8 268.3 %copy-start = (f32[3,4,8,64]{3,2,1,0:T(8,128)}, f32[3,4,8,64]{3,2,1,0:T(8,128)S(1)}, u32[]{:S(2)}) copy-start(f32[3,4,8,64]{3,2,1,0:T(8,128)S(1)} %add.174) | copy-start | bytes 73732
  191.5 1.7 collective-permute-start
  192.0 10.3 %copy-start.3 = (f32[4,8,64]{2,1,0:T(8,128)S(1)}, f32[4,8,64]{2,1,0:T(8,128)}, u32[]{:S(2)}) copy-start(f32[4,8,64]{2,1,0:T(8,128)} %get-tuple-element.415) | copy-start | bytes 24580
  192.0 3.6 collective-permute-start.1
  196.4 5.3 %collective-permute-start.2 = (f32[7,8,2,64]{3,2,1,0:T(2,128)S(1)}, f32[7,8,2,64]{3,2,1,0:T(2,128)S(1)}, u32[]{:S(2)}, u32[]{:S(2)}) collective-permute-start(f32[7,8,2,64]{3,2,1,0:T(2,128)S(1)} %get-tuple-element.176), channel_id=1, source_target_pairs={{0,1},{1,2},{2,3},{3,0},{4,5},{5,6},{6,7},{7,4},{8,9},{9,10},{10,1... | collective-permute-start | bytes 86024 | tf_op jit(solution)/shard_map/ppermute | solution.py:21
  198.3 4.1 collective-permute-start.3
  203.5 249.1 %collective-permute-start.4 = (f32[7,2,8,64]{3,2,1,0:T(8,128)S(1)}, f32[7,2,8,64]{3,2,1,0:T(8,128)S(1)}, u32[]{:S(2)}, u32[]{:S(2)}) collective-permute-start(f32[7,2,8,64]{3,2,1,0:T(8,128)S(1)} %get-tuple-element.178), channel_id=1, source_target_pairs={{0,4},{4,8},{8,12},{12,16},{16,20},{20,24},{24,28},{28,32},{32,36}... | collective-permute-start | bytes 86024 | tf_op jit(solution)/shard_map/ppermute | solution.py:21
  205.8 246.8 %collective-permute-start.5 = (f32[7,2,8,64]{3,2,1,0:T(8,128)S(1)}, f32[7,2,8,64]{3,2,1,0:T(8,128)S(1)}, u32[]{:S(2)}, u32[]{:S(2)}) collective-permute-start(f32[7,2,8,64]{3,2,1,0:T(8,128)S(1)} %get-tuple-element.179), channel_id=1, source_target_pairs={{4,0},{8,4},{12,8},{16,12},{20,16},{24,20},{28,24},{32,28},{36,32}... | collective-permute-start | bytes 86024 | tf_op jit(solution)/shard_map/ppermute | solution.py:24
  452.7 6.4 %collective-permute-start.6 = (f32[7,8,2,64]{3,2,1,0:T(2,128)S(1)}, f32[7,8,2,64]{3,2,1,0:T(2,128)S(1)}, u32[]{:S(2)}, u32[]{:S(2)}) collective-permute-start(f32[7,8,2,64]{3,2,1,0:T(2,128)S(1)} %get-tuple-element.174), channel_id=1, source_target_pairs={{0,1},{1,2},{2,3},{3,0},{4,5},{5,6},{6,7},{7,4},{8,9},{9,10},{10,1... | collective-permute-start | bytes 86024 | tf_op jit(solution)/shard_map/ppermute | solution.py:21
  453.6 5.5 %collective-permute-start.7 = (f32[7,8,2,64]{3,2,1,0:T(2,128)S(1)}, f32[7,8,2,64]{3,2,1,0:T(2,128)S(1)}, u32[]{:S(2)}, u32[]{:S(2)}) collective-permute-start(f32[7,8,2,64]{3,2,1,0:T(2,128)S(1)} %get-tuple-element.175), channel_id=1, source_target_pairs={{1,0},{2,1},{3,2},{0,3},{5,4},{6,5},{7,6},{4,7},{9,8},{10,9},{11,1... | collective-permute-start | bytes 86024 | tf_op jit(solution)/shard_map/ppermute | solution.py:24
Sparse Core Ops, SparseCore 0:
  201.1 250.5 all-reduce.1
